TPU v7x, 32 devices: a whole 2x2x4 slice. The times are simulated.
32 devices in a mesh: survey: 2 (over x), chan: 16 (over z, y, core).
Axes of the slice: x: 2, y: 2, z: 4, core: 2. Of those that a mesh axis runs over, the one named last changes fastest.
Arguments:
- das_window: float32 [8192, 8192], P(('survey', 'chan')), parts along dimension 0, may hold values from -6 to 6
- fan_bound: int32 [4096], replicated, may hold values from -1 to 2048, as said below
- tap_offset: int32 [8, 32], replicated, may hold values from -31 to 31, as said below
- tap_weight: float32 [8, 32], replicated, may hold values from -1 to 1
Outputs:
- filtered: float32 [8192, 8192], P(('survey', 'chan')), parts along dimension 0
- energy: float32 [8192, 8, 128], P(('survey', 'chan')), parts along dimension 0
There are 2 independent parts, one for each index of `survey`. A program takes and returns all parts, laid end to end along the dimension named above; an argument that names none is the same for every part. Nothing has to cross between parts.
Inputs may be any that keep to these rules, and one draw needn't show every extreme that they name: `fan_bound`: entry f bounds the magnitude of the signed channel wavenumber bin passed at the time frequency bins +f and -f; -1 passes none. `tap_offset`: the channel offset of a tap relative to the output channel.
All inputs are finite; a program needn't handle non-finite values.
Results may differ from a plain program's by a relative error of at most 0.0027.
Values may be sent and summed in bfloat16 or wider, within the bound.
No kernel may reach another device: no remote copies, remote signals or barrier semaphores. Data moves between devices by JAX's collectives and lax.ppermute only.
A program may use at most 256 MiB of HBM per device.

v0:
```python
import math
import jax
import jax.numpy as jnp
from jax import lax
from jax.sharding import PartitionSpec as P

HALO = 31
WIN = 64
PRECISE = lax.Precision.HIGHEST


def padded_2(value, sides, width):
    for axis, dim in sides:
        peers, length = (lax.axis_size(axis), value.shape[dim])
        up = [(i, (i + 1) % peers) for i in range(peers - 1)]
        down = [(j, i) for i, j in up]
        last = lax.slice_in_dim(value, length - width, length, axis=dim)
        leading = lax.slice_in_dim(value, 0, width, axis=dim)
        before = lax.ppermute(last, axis, up)
        after = lax.ppermute(leading, axis, down)
        value = jnp.concatenate([before, value, after], axis=dim)
    return value


def split_length(length_all):
    leading = 1
    while length_all % (4 * leading) == 0 and 4 * leading * leading <= length_all:
        leading = leading * 2
    return (leading, length_all // leading)


def phases(index_product, modulus, direction):
    angle = (index_product % modulus).astype(jnp.float32) * (2.0 * math.pi / modulus)
    return (jnp.cos(angle), direction * jnp.sin(angle))


def complex_table(real_part, imag_part, q_axis):
    first_row = jnp.stack([real_part, imag_part], axis=q_axis)
    second_row = jnp.stack([-imag_part, real_part], axis=q_axis)
    return jnp.stack([first_row, second_row], axis=0)


def square_phases(leading, direction):
    left_index = lax.broadcasted_iota(jnp.int32, (leading, leading), 0)
    right_index = lax.broadcasted_iota(jnp.int32, (leading, leading), 1)
    return phases(left_index * right_index, leading, direction)


def folded_table(shape_three, bin_axis, inner_axis, leading, modulus, direction):
    bin_index = lax.broadcasted_iota(jnp.int32, shape_three, bin_axis)
    outer_index = lax.broadcasted_iota(jnp.int32, shape_three, 3 - bin_axis - inner_axis)
    inner_index = lax.broadcasted_iota(jnp.int32, shape_three, inner_axis)
    return phases(inner_index * (bin_index + leading * outer_index), modulus, direction)


def time_forward(signal, kept_bins):
    row_count, sample_count = signal.shape
    leading, trailing = split_length(sample_count)
    used_bins = kept_bins // leading
    shaped = signal.reshape(row_count, leading, trailing)
    cos_first, sin_first = square_phases(leading, -1.0)
    first_table = jnp.stack([cos_first, sin_first], axis=1)
    first = jnp.einsum("rab,apk->rpkb", shaped, first_table, precision=PRECISE)
    cos_second, sin_second = folded_table(
        (leading, trailing, used_bins), 0, 1, leading, sample_count, -1.0
    )
    second_table = complex_table(cos_second, sin_second, 2)
    out = jnp.einsum("rpkb,pkbqm->rqmk", first, second_table, precision=PRECISE)
    return out.reshape(row_count, 2, kept_bins)


def channel_transform(field, direction):
    length_all, parts_count, column_count = field.shape
    leading, trailing = split_length(length_all)
    shaped = field.reshape(leading, trailing, parts_count, column_count)
    cos_first, sin_first = square_phases(leading, direction)
    first_table = complex_table(cos_first, sin_first, 1)
    first = jnp.einsum("abpn,paqk->kbqn", shaped, first_table, precision=PRECISE)
    cos_second, sin_second = folded_table(
        (leading, trailing, trailing), 0, 1, leading, length_all, direction
    )
    second_table = complex_table(cos_second, sin_second, 2)
    out = jnp.einsum("kbpn,pkbqm->mkqn", first, second_table, precision=PRECISE)
    return out.reshape(length_all, parts_count, column_count)


def time_inverse(spectrum, sample_count):
    row_count, parts_count, bin_count = spectrum.shape
    leading, trailing = split_length(sample_count)
    used_bins = bin_count // leading
    shaped = spectrum.reshape(row_count, parts_count, used_bins, leading)
    cos_first, sin_first = folded_table(
        (leading, used_bins, trailing), 0, 2, leading, sample_count, 1.0
    )
    first_table = complex_table(cos_first, sin_first, 2)
    first = jnp.einsum("rpmk,pkmqb->rqkb", shaped, first_table, precision=PRECISE)
    cos_last, sin_last = square_phases(leading, 1.0)
    last_table = jnp.stack([cos_last, -sin_last], axis=0)
    signal = jnp.einsum("rqkb,qka->rab", first, last_table, precision=PRECISE)
    signal = signal.reshape(row_count, sample_count)
    signal = 2.0 * signal - spectrum[:, 0, 0:1]
    return signal / sample_count


def per_device(das_window, fan_bound, tap_offset, tap_weight):
    row_count, sample_count = das_window.shape
    devices = lax.axis_size("chan")
    channel_count = row_count * devices
    kept_bins = sample_count // 2
    block_bins = kept_bins // devices
    spectrum = time_forward(das_window, kept_bins)
    by_freq = lax.all_to_all(spectrum, "chan", split_axis=2, concat_axis=0, tiled=True)
    wave = channel_transform(by_freq, -1.0)
    wave_index = lax.broadcasted_iota(jnp.int32, (channel_count, 1), 0)
    wave_signed = jnp.where(wave_index < channel_count // 2, wave_index, wave_index - channel_count)
    position = lax.axis_index("chan")
    extended = jnp.concatenate([fan_bound, jnp.full((1,), -1, jnp.int32)])
    limits = lax.dynamic_slice_in_dim(extended, position * block_bins, block_bins)
    passing = (jnp.abs(wave_signed) <= limits[None, :]).astype(jnp.float32)
    back = channel_transform(wave * passing[:, None, :], 1.0) / channel_count
    by_channel = lax.all_to_all(back, "chan", split_axis=0, concat_axis=2, tiled=True)
    filtered = time_inverse(by_channel, sample_count)
    low_field = filtered.astype(jnp.bfloat16)
    padded = padded_2(low_field, (("chan", 0),), HALO)
    span_count = 2 * HALO + 1
    offsets_grid = jnp.arange(span_count, dtype=jnp.int32) - HALO
    matches = (tap_offset[:, :, None] == offsets_grid[None, None, :]).astype(jnp.float32)
    kernel_low = jnp.sum(tap_weight[:, :, None] * matches, axis=1).astype(jnp.bfloat16)
    template_count = kernel_low.shape[0]
    piece_rows = 64
    offset_index = lax.broadcasted_iota(
        jnp.int32, (span_count, piece_rows, piece_rows + 2 * HALO), 0
    )
    output_index = lax.broadcasted_iota(
        jnp.int32, (span_count, piece_rows, piece_rows + 2 * HALO), 1
    )
    input_index = lax.broadcasted_iota(
        jnp.int32, (span_count, piece_rows, piece_rows + 2 * HALO), 2
    )
    selector = (input_index - output_index == offset_index).astype(jnp.bfloat16)
    stacking = jnp.einsum("ko,ori->rki", kernel_low, selector, preferred_element_type=jnp.float32)
    stacking = stacking.astype(jnp.bfloat16).reshape(
        piece_rows * template_count, piece_rows + 2 * HALO
    )

    def one_piece(first_row):
        window_rows = lax.dynamic_slice_in_dim(padded, first_row, piece_rows + 2 * HALO, 0)
        detection = jnp.dot(stacking, window_rows, preferred_element_type=jnp.float32)
        squared = (detection * detection).reshape(
            piece_rows * template_count, sample_count // WIN, WIN
        )
        return jnp.mean(squared, axis=2).reshape(piece_rows, template_count, sample_count // WIN)

    starts = jnp.arange(0, row_count, piece_rows, dtype=jnp.int32)
    energy = lax.map(one_piece, starts).reshape(row_count, template_count, sample_count // WIN)
    return (filtered, energy)


def solution(mesh):
    return jax.shard_map(
        per_device,
        mesh=mesh,
        in_specs=(P(("survey", "chan"), None), P(), P(), P()),
        out_specs=(P(("survey", "chan"), None), P(("survey", "chan"), None, None)),
        check_vma=False,
    )
```

profile of v0, /device:TPU:17, one launch (start us, length us, event | category | flops | bytes accessed | tf_op | source)
XLA Modules:
  0.0 740.6 jit_solution(12700331765586824724)
XLA Ops:
  0.8 8.4 %sine_multiply_fusion = (f32[64,128,1,64]{1,3,2,0:T(8,128)S(1)}, f32[64,128,1,64]{1,3,2,0:T(8,128)S(1)}, f32[64,128,1,64]{1,3,2,0:T(8,128)S(1)}) fusion(s32[64]{0:T(128)S(1)} %iota_multiply_fusion.1), kind=kLoop, calls=%fused_computation.74 | loop fusion | flops 8912896 | bytes 6291712 | tf_op jit(solution)/shard_map/mul | solution.py:34
  9.2 5.0 copy.102
  14.3 4.3 maximum_bitcast_fusion.2
  18.6 16.0 %convolution_bitcast_fusion.1 = f32[256,2,64,128,1]{3,2,0,1,4:T(8,128)} fusion(f32[256,64,128,1]{2,1,0,3:T(8,128)S(1)} %bitcast.148, f32[64,1,64]{0,2,1:T(8,128)S(1)} %get-tuple-element.68, f32[64,1,64]{0,2,1:T(8,128)S(1)} %get-tuple-element.67), kind=kOutput, calls=%fused_computation.37 | convolution fusion | flops 3221233664 | bytes 25198592 | tf_op jit(solution)/shard_map/rab,apk->rpkb/dot_general | solution.py:63
  34.6 33.7 %fusion.37 = f32[256,2,64,64]{0,2,1,3:T(8,128)S(1)} fusion(f32[256,2,64,128,1]{3,2,0,1,4:T(8,128)} %convolution_bitcast_fusion.1, f32[1,64,128,2,64]{2,4,0,3,1:T(8,128)} %get-tuple-element.51, f32[1,64,128,2,64]{2,4,0,3,1:T(8,128)} %get-tuple-element.50), kind=kOutput, calls=%fused_computation.54 | convolution fusion | flops 6444548096 | bytes 33554432 | tf_op jit(solution)/shard_map/rpkb,pkbqm->rqmk/dot_general | solution.py:68
  68.3 4.9 copy.56
  73.1 23.4 %copy.57 = f32[256,2,4096]{0,1,2:T(2,128)} copy(f32[256,2,4096]{0,2,1:T(8,128)S(1)} %bitcast.153) | data formatting | bytes 16777216 | tf_op jit(solution)/shard_map/reshape | solution.py:69
  96.6 6.9 all-to-all-start
  104.0 2.3 compare_convert_fusion
  106.3 8.5 %broadcast_multiply_fusion.1 = (f32[64,64,1,64]{1,3,0,2:T(8,128)S(1)}, f32[64,64,1,64]{1,3,0,2:T(8,128)S(1)}, f32[64,64,1,64]{1,3,0,2:T(8,128)S(1)}, f32[64,64,1,64]{1,3,0,2:T(8,128)S(1)}, f32[64,64,1,64]{1,3,0,2:T(8,128)S(1)}) fusion(s32[64]{0:T(128)S(1)} %iota_multiply_fusion.1), kind=kLoop, calls=%fused_computation.83 | loop fusion | flops 4718592 | bytes 5243136 | tf_op jit(solution)/shard_map/mul | solution.py:34
  114.8 7.4 fusion.30
  122.1 163.3 %all-to-all-done = f32[256,2,4096]{0,1,2:T(2,128)} async-done(((f32[256,2,4096]{0,1,2:T(2,128)}), f32[256,2,4096]{0,1,2:T(2,128)}, u32[]{:S(2)}, u32[]{:S(2)}) %all-to-all-start) | async-done | bytes 8388640 | tf_op jit(solution)/shard_map/all_to_all | solution.py:112
  285.4 7.4 %copy.58 = f32[256,2,4096]{0,2,1:T(8,128)} copy(f32[256,2,4096]{0,1,2:T(2,128)} %all-to-all-done) | data formatting | bytes 16777216 | tf_op jit(solution)/shard_map/all_to_all | solution.py:112
  292.9 8.7 %copy.59 = f32[16,256,2,256]{3,1,0,2:T(8,128)} copy(f32[16,256,2,256]{1,3,0,2:T(8,128)} %bitcast.154) | data formatting | bytes 16777216 | tf_op jit(solution)/shard_map/all_to_all | solution.py:112
  301.6 17.6 %fusion.31 = f32[64,64,2,256,1]{3,0,1,2,4:T(8,128)} fusion(f32[64,64,2,256]{3,1,0,2:T(8,128)} %bitcast.152, f32[1,64,2,64]{1,3,2,0:T(8,128)S(1)} %get-tuple-element.53, f32[1,64,2,64]{1,3,2,0:T(8,128)S(1)} %get-tuple-element.54), kind=kOutput, calls=%fused_computation.52 | convolution fusion | flops 3221241856 | bytes 16842752 | tf_op jit(solution)/shard_map/abpn,paqk->kbqn/dot_general | solution.py:78
  319.2 22.0 %fusion.20 = f32[64,2,64,256,1]{3,2,1,0,4:T(8,128)} fusion(f32[64,64,2,256,1]{3,0,1,2,4:T(8,128)} %fusion.31, f32[1,64,64,2,64]{2,4,1,3,0:T(8,128)} %get-tuple-element.47, f32[1,64,64,2,64]{2,4,1,3,0:T(8,128)} %get-tuple-element.46), kind=kOutput, calls=%fused_computation.30 | convolution fusion | flops 3222274048 | bytes 20971520 | tf_op jit(solution)/shard_map/kbpn,pkbqm->mkqn/dot_general | solution.py:83
  341.3 11.9 %fusion.34 = f32[64,64,2,256,1]{3,0,1,2,4:T(8,128)} fusion(f32[64,2,64,256,1]{3,2,1,0,4:T(8,128)} %fusion.20, f32[64,64,256]{2,0,1:T(8,128)S(1)} %copy-done.1, f32[1,64,2,64]{1,3,2,0:T(8,128)S(1)} %get-tuple-element.55, f32[1,64,2,64]{1,3,2,0:T(8,128)S(1)} %get-tuple-element.52), kind=kOutput, calls=%fused_computation.53 | convolution fusion | flops 3223339008 | bytes 21037056 | tf_op jit(solution)/shard_map/abpn,paqk->kbqn/dot_general | solution.py:78
  353.2 22.1 %fusion.8 = f32[64,2,64,256,1]{3,2,0,1,4:T(8,128)} fusion(f32[1,64,64,2,64]{2,4,1,3,0:T(8,128)} %get-tuple-element.48, f32[1,64,64,2,64]{2,4,1,3,0:T(8,128)} %get-tuple-element.49, f32[64,64,2,256,1]{3,0,1,2,4:T(8,128)} %fusion.34), kind=kOutput, calls=%fused_computation.14 | convolution fusion | flops 3222274048 | bytes 20971520 | tf_op jit(solution)/shard_map/kbpn,pkbqm->mkqn/dot_general | solution.py:83
  375.3 4.3 fusion.16
  379.6 4.9 copy.67
  384.4 23.4 %copy.68 = f32[4096,2,256]{2,1,0:T(2,128)} copy(f32[4096,2,256]{2,0,1:T(8,128)S(1)} %bitcast.155) | data formatting | bytes 16777216 | tf_op jit(solution)/shard_map/div | solution.py:120
  407.9 5.2 all-to-all-start.1
  413.2 8.4 %fusion.55 = (f32[64,64,1,128]{3,1,2,0:T(8,128)S(1)}, f32[64,64,1,128]{3,1,2,0:T(8,128)S(1)}, f32[64,64,1,128]{3,1,2,0:T(8,128)S(1)}) fusion(s32[64]{0:T(128)S(1)} %iota_multiply_fusion.1), kind=kLoop, calls=%fused_computation.79 | loop fusion | flops 8388608 | bytes 6291712 | tf_op jit(solution)/shard_map/sin | solution.py:34
  421.7 4.2 maximum_bitcast_fusion
  425.9 169.3 %all-to-all-done.1 = f32[4096,2,256]{2,1,0:T(2,128)} async-done(((f32[4096,2,256]{2,1,0:T(2,128)}), f32[4096,2,256]{2,1,0:T(2,128)}, u32[]{:S(2)}, u32[]{:S(2)}) %all-to-all-start.1) | async-done | bytes 8388640 | tf_op jit(solution)/shard_map/all_to_all | solution.py:121
  595.2 7.4 %copy.69 = f32[4096,2,256]{2,0,1:T(8,128)} copy(f32[4096,2,256]{2,1,0:T(2,128)} %all-to-all-done.1) | data formatting | bytes 16777216 | tf_op jit(solution)/shard_map/all_to_all | solution.py:121
  602.6 8.7 %copy.70 = f32[256,2,16,256]{0,3,2,1:T(8,128)} copy(f32[256,2,16,256]{3,0,2,1:T(8,128)} %bitcast.156) | data formatting | bytes 16777216 | tf_op jit(solution)/shard_map/all_to_all | solution.py:121
  611.3 31.8 %convolution_bitcast_fusion = f32[256,2,64,128]{0,3,1,2:T(8,128)} fusion(f32[1,64,64,2,128]{4,2,0,3,1:T(8,128)} %get-tuple-element.45, f32[1,64,64,2,128]{4,2,0,3,1:T(8,128)} %get-tuple-element.44, f32[256,2,64,64,1]{0,3,2,1,4:T(8,128)} %bitcast.149), kind=kOutput, calls=%fused_computation.8 | convolution fusion | flops 6444548096 | bytes 33554432 | tf_op jit(solution)/shard_map/rpmk,pkmqb->rqkb/dot_general | solution.py:96
  643.1 16.8 %copy.72 = f32[256,2,64,128]{3,2,1,0:T(8,128)} copy(f32[256,2,64,128]{0,3,1,2:T(8,128)} %convolution_bitcast_fusion) | data formatting | bytes 33554432 | tf_op jit(solution)/shard_map/rpmk,pkmqb->rqkb/transpose | solution.py:96
  659.9 0.7 slice.12
  660.6 12.2 %bitcast_multiply_fusion.1 = f32[64,256,128]{2,0,1:T(8,128)S(1)} fusion(f32[256,2,64,128]{3,2,1,0:T(8,128)} %copy.72, f32[1,64,64]{1,2,0:T(8,128)S(1)} %get-tuple-element.71, f32[1,64,64]{1,2,0:T(8,128)S(1)} %get-tuple-element.72), kind=kOutput, calls=%fused_computation.23 | convolution fusion | flops 3223330816 | bytes 25198592 | tf_op jit(solution)/shard_map/rqkb,qka->rab/dot_general | solution.py:99
  672.8 11.9 %fusion.98 = (bf16[256,8192]{1,0:T(8,128)(2,1)S(1)}, f32[256,8192]{1,0:T(8,128)}) fusion(f32[256]{0:T(256)S(1)} %bitcast.158, f32[32,8,64,128]{3,2,1,0:T(8,128)S(1)} %bitcast.151), kind=kLoop, calls=%fused_computation.144 | loop fusion | flops 6291456 | bytes 20972544 | tf_op jit(solution)/shard_map/convert_element_type | solution.py:123
  684.7 2.0 copy-done
  686.8 2.0 collective-permute-start
  688.9 2.7 collective-permute-start.1
  692.2 8.4 %collective-permute-done = bf16[31,8192]{1,0:T(8,128)(2,1)S(1)} collective-permute-done((bf16[31,8192]{1,0:T(8,128)(2,1)S(1)}, bf16[31,8192]{1,0:T(8,128)(2,1)S(1)}, u32[]{:S(2)}, u32[]{:S(2)}) %collective-permute-start) | collective-permute-done | bytes 507936 | tf_op jit(solution)/shard_map/ppermute | solution.py:19
  700.6 3.4 collective-permute-done.1
  704.0 6.4 pad_maximum_fusion.1
  710.4 29.7 %while.10 = (s32[]{:T(128)}, f32[4,64,8,128]{3,2,1,0:T(8,128)}, s32[4]{0:T(128)S(1)}, bf16[318,8192]{1,0:T(8,128)(2,1)}, bf16[512,126]{1,0:T(8,128)(2,1)S(1)}, /*index=5*/s32[]{:T(128)}, s32[]{:T(128)}, s32[]{:T(128)}) while((s32[]{:T(128)}, f32[4,64,8,128]{3,2,1,0:T(8,128)}, s32[4]{0:T(128)S(1)}, bf16[318,8192]{1,0:T(8,128)(2,1)}, ...), condition=%wide.region_3.4_spmd, body=%wide.region_1.3_spmd.sunk | while | flops 1065353216 | bytes 4061831 | solution.py:155
  710.4 0.6 dynamic_slice.22
  712.9 4.0 bitcast_reduce_fusion.2
  717.1 0.7 bitcast_dynamic-update-slice_fusion.2
  720.4 4.1 bitcast_reduce_fusion.2
  724.6 0.7 bitcast_dynamic-update-slice_fusion.2
  727.8 4.0 bitcast_reduce_fusion.2
  732.0 0.7 bitcast_dynamic-update-slice_fusion.2
  735.2 4.0 bitcast_reduce_fusion.2
  739.4 0.7 bitcast_dynamic-update-slice_fusion.2
  (34 shorter events, 4.0 us)
Async XLA Ops:
  96.6 7.0 copy-start.2
  96.6 188.8 %all-to-all-start = ((f32[256,2,4096]{0,1,2:T(2,128)}), f32[256,2,4096]{0,1,2:T(2,128)}, u32[]{:S(2)}, u32[]{:S(2)}) async-start(f32[256,2,4096]{0,1,2:T(2,128)} %copy.57), calls=%async_computation | async-start | bytes 16777216 | tf_op jit(solution)/shard_map/all_to_all | solution.py:112
  319.2 22.1 %copy-start.1 = (f32[64,64,256]{2,0,1:T(8,128)S(1)}, f32[64,64,256]{2,0,1:T(8,128)}, u32[]{:S(2)}) copy-start(f32[64,64,256]{2,0,1:T(8,128)} %compare_convert_fusion) | copy-start | bytes 12582916
  407.9 187.3 %all-to-all-start.1 = ((f32[4096,2,256]{2,1,0:T(2,128)}), f32[4096,2,256]{2,1,0:T(2,128)}, u32[]{:S(2)}, u32[]{:S(2)}) async-start(f32[4096,2,256]{2,1,0:T(2,128)} %copy.68), calls=%async_computation.1 | async-start | bytes 16777216 | tf_op jit(solution)/shard_map/all_to_all | solution.py:121
  672.8 18.8 %copy-start.3 = (f32[8,32]{1,0:T(8,128)S(1)}, f32[8,32]{1,0:T(8,128)}, u32[]{:S(2)}) copy-start(f32[8,32]{1,0:T(8,128)} %param.9) | copy-start | bytes 3076
  672.8 18.8 %copy-start.4 = (s32[8,32]{1,0:T(8,128)S(1)}, s32[8,32]{1,0:T(8,128)}, u32[]{:S(2)}) copy-start(s32[8,32]{1,0:T(8,128)} %param.8) | copy-start | bytes 3076
  684.7 2.0 copy-start
  686.8 13.8 %collective-permute-start = (bf16[31,8192]{1,0:T(8,128)(2,1)S(1)}, bf16[31,8192]{1,0:T(8,128)(2,1)S(1)}, u32[]{:S(2)}, u32[]{:S(2)}) collective-permute-start(bf16[31,8192]{1,0:T(8,128)(2,1)S(1)} %get-tuple-element.42), channel_id=1, source_target_pairs={{0,1},{1,2},{2,3},{3,4},{4,5},{5,6},{6,7},{7,8},{8,9},{9,10},{10,1... | collective-permute-start | bytes 1523720 | tf_op jit(solution)/shard_map/ppermute | solution.py:19
  688.9 15.2 %collective-permute-start.1 = (bf16[31,8192]{1,0:T(8,128)(2,1)S(1)}, bf16[31,8192]{1,0:T(8,128)(2,1)S(1)}, u32[]{:S(2)}, u32[]{:S(2)}) collective-permute-start(bf16[31,8192]{1,0:T(8,128)(2,1)S(1)} %get-tuple-element.43), channel_id=1, source_target_pairs={{1,0},{2,1},{3,2},{4,3},{5,4},{6,5},{7,6},{8,7},{9,8},{10,9},{11,1... | collective-permute-start | bytes 1523720 | tf_op jit(solution)/shard_map/ppermute | solution.py:20
where the time goes:
time: 750 us; the launch traced here: 741 us
  waiting for transfers between devices  344 us (46%)
  matrix products  184 us (25%)
  local copies, waits for them, and re-layouts  120 us (16%)
  other arithmetic  67 us (9%)
  starting transfers between devices  16.9 us (2%)
  loops' own time  7.54 us (1%)
    all_to_all x1, waiting for transfers between devices, per_device(): lax.all_to_all(back, 'chan', split_axis=0, concat_axis=2, tiled=True)  169 us
    all_to_all x1, waiting for transfers between devices, per_device(): lax.all_to_all(spectrum, 'chan', split_axis=2, concat_axis=0, tiled=True)  163 us
    dot_general x2, matrix products, channel_transform(): out = jnp.einsum('kbpn,pkbqm->mkqn', first, second_table, precision=PRECISE)  44.2 us
    dot_general x1, matrix products, time_forward(): out = jnp.einsum('rpkb,pkbqm->rqmk', first, second_table, precision=PRECISE)  33.7 us
    dot_general x1, matrix products, time_inverse(): jnp.einsum('rpmk,pkmqb->rqkb', shaped, first_table, precision=PRECISE)  31.8 us
    dot_general x2, matrix products, channel_transform(): jnp.einsum('abpn,paqk->kbqn', shaped, first_table, precision=PRECISE)  29.5 us
    div x2, local copies, waits for them, and re-layouts, per_device(): back = channel_transform(wave * passing[:, None, :], 1.0) / channel_count  28.3 us
    reshape x1, local copies, waits for them, and re-layouts, time_forward(): return out.reshape(row_count, 2, kept_bins)  23.4 us
  transfers between devices with their start and end apart: 4, of which 4 were waited for; matrix products, arithmetic and copies ran while one was open for 4% of the time, Pallas kernels for 0%

commit v1 on v0

--- a/solution.py
+++ b/solution.py
@@ -7,6 +7,18 @@
 HALO = 31
 WIN = 64
 PRECISE = lax.Precision.HIGHEST
+
+
+def split_up(x, dim, devices):
+    dims = x.shape
+    parts = x.reshape(*dims[:dim], devices, dims[dim] // devices, *dims[dim + 1 :])
+    return jnp.moveaxis(parts, dim, 0)
+
+
+def joined_along(blocks, dim):
+    dims = list(blocks.shape[1:])
+    dims[dim] *= blocks.shape[0]
+    return jnp.moveaxis(blocks, 0, dim).reshape(dims)
 
 
 def padded_2(value, sides, width):
@@ -109,7 +121,14 @@
     kept_bins = sample_count // 2
     block_bins = kept_bins // devices
     spectrum = time_forward(das_window, kept_bins)
-    by_freq = lax.all_to_all(spectrum, "chan", split_axis=2, concat_axis=0, tiled=True)
+    size, index = (lax.axis_size("chan"), lax.axis_index("chan"))
+    tiles = split_up(spectrum, 2, size)
+    outs = [tiles[index]]
+    for lap in range(1, size):
+        sent = tiles[index ^ lap]
+        outs.append(lax.ppermute(sent, "chan", [(i_2, i_2 ^ lap) for i_2 in range(size)]))
+    tiles = jnp.stack(outs)[index ^ jnp.arange(size)]
+    by_freq = joined_along(tiles, 0)
     wave = channel_transform(by_freq, -1.0)
     wave_index = lax.broadcasted_iota(jnp.int32, (channel_count, 1), 0)
     wave_signed = jnp.where(wave_index < channel_count // 2, wave_index, wave_index - channel_count)

time: 750 us -> 776 us (1.035)
  starting transfers between devices: 16.9 us -> 35.7 us
  local copies, waits for them, and re-layouts: 120 us -> 137 us
  waiting for transfers between devices: 344 us -> 332 us
    all_to_all x1 -> x0, waiting for transfers between devices: 163 us -> none  [per_device(): lax.all_to_all(spectrum, 'chan', split_axis=2, concat_axis=0, tiled=True)]
    ppermute x0 -> x15, waiting for transfers between devices: none -> 152 us  [per_device(): lax.ppermute(sent, 'chan', [(i_2, i_2 ^ lap) for i_2 in range(size)])]
    ppermute x0 -> x15, starting transfers between devices: none -> 26.3 us  [per_device(): lax.ppermute(sent, 'chan', [(i_2, i_2 ^ lap) for i_2 in range(size)])]
    reshape x1 -> x0, local copies, waits for them, and re-layouts: 23.4 us -> none  [time_forward(): return out.reshape(row_count, 2, kept_bins)]
    another operation x0 -> x18, local copies, waits for them, and re-layouts: none -> 23.3 us
    unnamed x11 -> x40, local copies, waits for them, and re-layouts: 7.04 us -> 25.9 us
    all_to_all x2 -> x0, local copies, waits for them, and re-layouts: 16.2 us -> none  [per_device(): lax.all_to_all(spectrum, 'chan', split_axis=2, concat_axis=0, tiled=True)]
    gather x0 -> x2, local copies, waits for them, and re-layouts: none -> 11.7 us  [per_device(): tiles = jnp.stack(outs)[index ^ jnp.arange(size)]]
  transfers between devices with their start and end apart: 4 -> 18, of which waited for: 4 -> 12; matrix products, arithmetic and copies ran while one was open for 4% -> 9% of each run, Pallas kernels for 0% -> 0%
where the time goes in v1:
time: 776 us; the launch traced here: 766 us
  waiting for transfers between devices  332 us (43%)
  matrix products  180 us (23%)
  local copies, waits for them, and re-layouts  137 us (18%)
  other arithmetic  71.3 us (9%)
  starting transfers between devices  35.7 us (5%)
  loops' own time  8.4 us (1%)
    all_to_all x1, waiting for transfers between devices, per_device(): lax.all_to_all(back, 'chan', split_axis=0, concat_axis=2, tiled=True)  169 us
    ppermute x15, waiting for transfers between devices, per_device(): lax.ppermute(sent, 'chan', [(i_2, i_2 ^ lap) for i_2 in range(size)])  152 us
    dot_general x2, matrix products, channel_transform(): out = jnp.einsum('kbpn,pkbqm->mkqn', first, second_table, precision=PRECISE)  44.3 us
    dot_general x1, matrix products, time_forward(): out = jnp.einsum('rpkb,pkbqm->rqmk', first, second_table, precision=PRECISE)  33.7 us
    dot_general x1, matrix products, time_inverse(): jnp.einsum('rpmk,pkmqb->rqkb', shaped, first_table, precision=PRECISE)  31.7 us
    div x2, local copies, waits for them, and re-layouts, per_device(): back = channel_transform(wave * passing[:, None, :], 1.0) / channel_count  28.3 us
    ppermute x15, starting transfers between devices, per_device(): lax.ppermute(sent, 'chan', [(i_2, i_2 ^ lap) for i_2 in range(size)])  26.3 us
    unnamed x40, local copies, waits for them, and re-layouts  25.9 us
  transfers between devices with their start and end apart: 18, of which 12 were waited for; matrix products, arithmetic and copies ran while one was open for 9% of the time, Pallas kernels for 0%

profile of v1, /device:TPU:17, one launch (start us, length us, event | category | flops | bytes accessed | tf_op | source)
XLA Modules:
  0.0 765.9 jit_solution(6404005559477305063)
XLA Ops:
  0.9 8.4 %sine_multiply_fusion = (f32[64,128,1,64]{1,3,2,0:T(8,128)S(1)}, f32[64,128,1,64]{1,3,2,0:T(8,128)S(1)}, f32[64,128,1,64]{1,3,2,0:T(8,128)S(1)}) fusion(s32[64]{0:T(128)S(1)} %iota_multiply_fusion.1), kind=kLoop, calls=%fused_computation.75 | loop fusion | flops 8912896 | bytes 6291712 | tf_op jit(solution)/shard_map/mul | solution.py:46
  9.3 5.0 copy.191
  14.3 4.3 maximum_bitcast_fusion.2
  18.7 16.0 %convolution_bitcast_fusion.1 = f32[256,2,64,128,1]{3,2,0,1,4:T(8,128)} fusion(f32[256,64,128,1]{2,1,0,3:T(8,128)S(1)} %bitcast.194, f32[64,1,64]{0,2,1:T(8,128)S(1)} %get-tuple-element.84, f32[64,1,64]{0,2,1:T(8,128)S(1)} %get-tuple-element.83), kind=kOutput, calls=%fused_computation.38 | convolution fusion | flops 3221233664 | bytes 25198592 | tf_op jit(solution)/shard_map/rab,apk->rpkb/dot_general | solution.py:75
  34.7 33.7 %fusion.37 = f32[256,2,64,64]{0,2,1,3:T(8,128)S(1)} fusion(f32[256,2,64,128,1]{3,2,0,1,4:T(8,128)} %convolution_bitcast_fusion.1, f32[1,64,128,2,64]{2,4,0,3,1:T(8,128)} %get-tuple-element.67, f32[1,64,128,2,64]{2,4,0,3,1:T(8,128)} %get-tuple-element.66), kind=kOutput, calls=%fused_computation.55 | convolution fusion | flops 6444548096 | bytes 33554432 | tf_op jit(solution)/shard_map/rpkb,pkbqm->rqmk/dot_general | solution.py:80
  68.4 8.3 %copy.131 = f32[256,2,64,64]{0,3,2,1:T(8,128)} copy(f32[256,2,64,64]{0,2,1,3:T(8,128)S(1)} %fusion.37) | data formatting | bytes 16777216 | tf_op jit(solution)/shard_map/rpkb,pkbqm->rqmk/transpose | solution.py:80
  76.6 5.9 constant_dynamic-slice_fusion
  91.7 10.2 %broadcast_multiply_fusion.1 = (f32[64,64,1,64]{1,3,0,2:T(8,128)S(1)}, f32[64,64,1,64]{1,3,0,2:T(8,128)}, f32[64,64,1,64]{1,3,0,2:T(8,128)}, f32[64,64,1,64]{1,3,0,2:T(8,128)}, f32[64,64,1,64]{1,3,0,2:T(8,128)}) fusion(s32[64]{0:T(128)S(1)} %iota_multiply_fusion.1), kind=kLoop, calls=%fused_computation.84 | loop fusion | flops 4718592 | bytes 5243136 | tf_op jit(solution)/shard_map/mul | solution.py:46
  107.8 9.6 %fusion.30 = (f32[1,64,64,2,64]{2,4,1,3,0:T(8,128)}, f32[1,64,64,2,64]{2,4,1,3,0:T(8,128)}, f32[1,64,64,2,64]{2,4,1,3,0:T(8,128)}, f32[1,64,64,2,64]{2,4,1,3,0:T(8,128)}) fusion(f32[64,64,1,64]{1,3,0,2:T(8,128)} %get-tuple-element.79, f32[64,64,1,64]{1,3,0,2:T(8,128)S(1)} %get-tuple-element.75, f32[64,64,1,64]{1,3,0,2:T(8,128)S(1)} %copy-done.2, ...), kind=kLoop, calls=%fused_computation.47 | loop fusion | flops 2097152 | bytes 13631488 | tf_op jit(solution)/shard_map/stack | solution.py:52
  143.9 14.3 %collective-permute-done.5 = f32[256,2,256]{2,0,1:T(8,128)S(1)} collective-permute-done((f32[256,2,256]{2,0,1:T(8,128)}, f32[256,2,256]{2,0,1:T(8,128)S(1)}, u32[]{:S(2)}, u32[]{:S(2)}) %collective-permute-start.5) | collective-permute-done | bytes 524320 | tf_op jit(solution)/shard_map/ppermute | solution.py:129
  158.3 5.1 collective-permute-start.10
  164.2 5.3 collective-permute-done.6
  173.6 51.2 %collective-permute-done.8 = f32[256,2,256]{2,0,1:T(8,128)S(1)} collective-permute-done((f32[256,2,256]{2,0,1:T(8,128)}, f32[256,2,256]{2,0,1:T(8,128)S(1)}, u32[]{:S(2)}, u32[]{:S(2)}) %collective-permute-start.8) | collective-permute-done | bytes 524320 | tf_op jit(solution)/shard_map/ppermute | solution.py:129
  224.7 3.3 collective-permute-start.13
  228.9 18.3 %collective-permute-done.9 = f32[256,2,256]{2,0,1:T(8,128)S(1)} collective-permute-done((f32[256,2,256]{2,0,1:T(8,128)}, f32[256,2,256]{2,0,1:T(8,128)S(1)}, u32[]{:S(2)}, u32[]{:S(2)}) %collective-permute-start.9) | collective-permute-done | bytes 524320 | tf_op jit(solution)/shard_map/ppermute | solution.py:129
  247.2 4.9 collective-permute-start.14
  253.0 16.6 %collective-permute-done.10 = f32[256,2,256]{2,0,1:T(8,128)S(1)} collective-permute-done((f32[256,2,256]{2,0,1:T(8,128)S(1)}, f32[256,2,256]{2,0,1:T(8,128)S(1)}, u32[]{:S(2)}, u32[]{:S(2)}) %collective-permute-start.10) | collective-permute-done | bytes 524320 | tf_op jit(solution)/shard_map/ppermute | solution.py:129
  270.4 13.5 %collective-permute-done.11 = f32[256,2,256]{2,0,1:T(8,128)S(1)} collective-permute-done((f32[256,2,256]{2,0,1:T(8,128)S(1)}, f32[256,2,256]{2,0,1:T(8,128)S(1)}, u32[]{:S(2)}, u32[]{:S(2)}) %collective-permute-start.11) | collective-permute-done | bytes 524320 | tf_op jit(solution)/shard_map/ppermute | solution.py:129
  284.8 11.4 %collective-permute-done.12 = f32[256,2,256]{2,0,1:T(8,128)S(1)} collective-permute-done((f32[256,2,256]{2,0,1:T(8,128)S(1)}, f32[256,2,256]{2,0,1:T(8,128)S(1)}, u32[]{:S(2)}, u32[]{:S(2)}) %collective-permute-start.12) | collective-permute-done | bytes 524320 | tf_op jit(solution)/shard_map/ppermute | solution.py:129
  297.0 10.4 %collective-permute-done.13 = f32[256,2,256]{2,0,1:T(8,128)S(1)} collective-permute-done((f32[256,2,256]{2,0,1:T(8,128)S(1)}, f32[256,2,256]{2,0,1:T(8,128)S(1)}, u32[]{:S(2)}, u32[]{:S(2)}) %collective-permute-start.13) | collective-permute-done | bytes 524320 | tf_op jit(solution)/shard_map/ppermute | solution.py:129
  308.2 10.8 %collective-permute-done.14 = f32[256,2,256]{2,0,1:T(8,128)S(1)} collective-permute-done((f32[256,2,256]{2,0,1:T(8,128)S(1)}, f32[256,2,256]{2,0,1:T(8,128)S(1)}, u32[]{:S(2)}, u32[]{:S(2)}) %collective-permute-start.14) | collective-permute-done | bytes 524320 | tf_op jit(solution)/shard_map/ppermute | solution.py:129
  319.8 7.7 %gather_fusion = f32[16,256,2,256]{3,1,2,0:T(8,128)} fusion(f32[16,256,2,256]{3,1,2,0:T(8,128)} %bitcast_dynamic-update-slice_fusion.1, s32[1024]{0:T(1024)S(1)} %pad_clamp_fusion), kind=kCustom, calls=%fused_computation | custom fusion | bytes 16777280 | tf_op jit(solution)/shard_map/gather | solution.py:130
  327.5 3.9 copy.148
  331.4 13.2 %fusion.31 = f32[64,64,2,256,1]{3,0,1,2,4:T(8,128)} fusion(f32[64,64,2,256]{3,1,0,2:T(8,128)S(1)} %bitcast.199, f32[1,64,2,64]{1,3,2,0:T(8,128)S(1)} %get-tuple-element.69, f32[1,64,2,64]{1,3,2,0:T(8,128)S(1)} %get-tuple-element.70), kind=kOutput, calls=%fused_computation.53 | convolution fusion | flops 3221241856 | bytes 16842752 | tf_op jit(solution)/shard_map/abpn,paqk->kbqn/dot_general | solution.py:90
  344.7 22.1 %fusion.20 = f32[64,2,64,256,1]{3,2,1,0,4:T(8,128)} fusion(f32[64,64,2,256,1]{3,0,1,2,4:T(8,128)} %fusion.31, f32[1,64,64,2,64]{2,4,1,3,0:T(8,128)} %get-tuple-element.63, f32[1,64,64,2,64]{2,4,1,3,0:T(8,128)} %get-tuple-element.62), kind=kOutput, calls=%fused_computation.31 | convolution fusion | flops 3222274048 | bytes 20971520 | tf_op jit(solution)/shard_map/kbpn,pkbqm->mkqn/dot_general | solution.py:95
  366.8 11.9 %fusion.34 = f32[64,64,2,256,1]{3,0,1,2,4:T(8,128)} fusion(f32[64,2,64,256,1]{3,2,1,0,4:T(8,128)} %fusion.20, f32[64,64,256]{2,0,1:T(8,128)S(1)} %copy-done.1, f32[1,64,2,64]{1,3,2,0:T(8,128)S(1)} %get-tuple-element.71, f32[1,64,2,64]{1,3,2,0:T(8,128)S(1)} %get-tuple-element.68), kind=kOutput, calls=%fused_computation.54 | convolution fusion | flops 3223339008 | bytes 21037056 | tf_op jit(solution)/shard_map/abpn,paqk->kbqn/dot_general | solution.py:90
  378.7 22.2 %fusion.8 = f32[64,2,64,256,1]{3,2,0,1,4:T(8,128)} fusion(f32[1,64,64,2,64]{2,4,1,3,0:T(8,128)} %get-tuple-element.64, f32[1,64,64,2,64]{2,4,1,3,0:T(8,128)} %get-tuple-element.65, f32[64,64,2,256,1]{3,0,1,2,4:T(8,128)} %fusion.34), kind=kOutput, calls=%fused_computation.15 | convolution fusion | flops 3222274048 | bytes 20971520 | tf_op jit(solution)/shard_map/kbpn,pkbqm->mkqn/dot_general | solution.py:95
  400.9 4.3 fusion.16
  405.2 4.9 copy.156
  410.0 23.4 %copy.157 = f32[4096,2,256]{2,1,0:T(2,128)} copy(f32[4096,2,256]{2,0,1:T(8,128)S(1)} %bitcast.200) | data formatting | bytes 16777216 | tf_op jit(solution)/shard_map/div | solution.py:139
  433.5 4.7 all-to-all-start
  438.3 8.4 %fusion.55 = (f32[64,64,1,128]{3,1,2,0:T(8,128)S(1)}, f32[64,64,1,128]{3,1,2,0:T(8,128)S(1)}, f32[64,64,1,128]{3,1,2,0:T(8,128)S(1)}) fusion(s32[64]{0:T(128)S(1)} %iota_multiply_fusion.1), kind=kLoop, calls=%fused_computation.80 | loop fusion | flops 8388608 | bytes 6291712 | tf_op jit(solution)/shard_map/sin | solution.py:46
  446.7 4.3 maximum_bitcast_fusion
  451.0 168.5 %all-to-all-done = f32[4096,2,256]{2,1,0:T(2,128)} async-done(((f32[4096,2,256]{2,1,0:T(2,128)}), f32[4096,2,256]{2,1,0:T(2,128)}, u32[]{:S(2)}, u32[]{:S(2)}) %all-to-all-start) | async-done | bytes 8388640 | tf_op jit(solution)/shard_map/all_to_all | solution.py:140
  619.5 7.4 copy.158
  627.0 8.7 %copy.159 = f32[256,2,16,256]{0,3,2,1:T(8,128)} copy(f32[256,2,16,256]{3,0,2,1:T(8,128)} %bitcast.201) | data formatting | bytes 16777216 | tf_op jit(solution)/shard_map/all_to_all | solution.py:140
  635.7 31.7 %convolution_bitcast_fusion = f32[256,2,64,128]{0,3,1,2:T(8,128)} fusion(f32[1,64,64,2,128]{4,2,0,3,1:T(8,128)} %get-tuple-element.61, f32[1,64,64,2,128]{4,2,0,3,1:T(8,128)} %get-tuple-element.60, f32[256,2,64,64,1]{0,3,2,1,4:T(8,128)} %bitcast.195), kind=kOutput, calls=%fused_computation.9 | convolution fusion | flops 6444548096 | bytes 33554432 | tf_op jit(solution)/shard_map/rpmk,pkmqb->rqkb/dot_general | solution.py:108
  667.4 16.9 %copy.161 = f32[256,2,64,128]{3,2,1,0:T(8,128)} copy(f32[256,2,64,128]{0,3,1,2:T(8,128)} %convolution_bitcast_fusion) | data formatting | bytes 33554432 | tf_op jit(solution)/shard_map/rpmk,pkmqb->rqkb/transpose | solution.py:108
  685.0 12.2 %bitcast_multiply_fusion.1 = f32[64,256,128]{2,0,1:T(8,128)S(1)} fusion(f32[256,2,64,128]{3,2,1,0:T(8,128)} %copy.161, f32[1,64,64]{1,2,0:T(8,128)S(1)} %get-tuple-element.87, f32[1,64,64]{1,2,0:T(8,128)S(1)} %get-tuple-element.88), kind=kOutput, calls=%fused_computation.24 | convolution fusion | flops 3223330816 | bytes 25198592 | tf_op jit(solution)/shard_map/rqkb,qka->rab/dot_general | solution.py:111
  697.2 11.9 %fusion.99 = (bf16[256,8192]{1,0:T(8,128)(2,1)S(1)}, f32[256,8192]{1,0:T(8,128)}) fusion(f32[256]{0:T(256)S(1)} %bitcast.214, f32[32,8,64,128]{3,2,1,0:T(8,128)S(1)} %bitcast.197), kind=kLoop, calls=%fused_computation.180 | loop fusion | flops 6291456 | bytes 20972544 | tf_op jit(solution)/shard_map/convert_element_type | solution.py:142
  716.6 8.4 %collective-permute-done.15 = bf16[31,8192]{1,0:T(8,128)(2,1)S(1)} collective-permute-done((bf16[31,8192]{1,0:T(8,128)(2,1)S(1)}, bf16[31,8192]{1,0:T(8,128)(2,1)S(1)}, u32[]{:S(2)}, u32[]{:S(2)}) %collective-permute-start.15) | collective-permute-done | bytes 507936 | tf_op jit(solution)/shard_map/ppermute | solution.py:31
  725.0 3.4 collective-permute-done.16
  728.4 6.4 pad_maximum_fusion.1
  734.8 30.7 %while.10 = (s32[]{:T(128)}, f32[4,64,8,128]{3,2,1,0:T(8,128)}, s32[4]{0:T(128)S(1)}, bf16[318,8192]{1,0:T(8,128)(2,1)}, bf16[512,126]{1,0:T(8,128)(2,1)S(1)}, /*index=5*/s32[]{:T(128)}, s32[]{:T(128)}, s32[]{:T(128)}) while((s32[]{:T(128)}, f32[4,64,8,128]{3,2,1,0:T(8,128)}, s32[4]{0:T(128)S(1)}, bf16[318,8192]{1,0:T(8,128)(2,1)}, ...), condition=%wide.region_3.4_spmd, body=%wide.region_1.3_spmd.sunk | while | flops 1065353216 | bytes 4061831 | solution.py:174
  737.5 4.1 bitcast_reduce_fusion.2
  745.2 4.0 bitcast_reduce_fusion.2
  752.9 4.0 bitcast_reduce_fusion.2
  760.6 4.0 bitcast_reduce_fusion.2
  (110 shorter events, 66.7 us)
Async XLA Ops:
  83.5 44.7 %collective-permute-start = (f32[256,2,256]{2,0,1:T(8,128)}, f32[256,2,256]{2,0,1:T(8,128)}, u32[]{:S(2)}, u32[]{:S(2)}) collective-permute-start(f32[256,2,256]{2,0,1:T(8,128)} %bitcast.209), channel_id=1, source_target_pairs={{0,1},{1,0},{2,3},{3,2},{4,5},{5,4},{6,7},{7,6},{8,9},{9,8},{10,11... | collective-permute-start | bytes 1572872 | tf_op jit(solution)/shard_map/ppermute | solution.py:129
  85.2 47.2 %collective-permute-start.1 = (f32[256,2,256]{2,0,1:T(8,128)}, f32[256,2,256]{2,0,1:T(8,128)}, u32[]{:S(2)}, u32[]{:S(2)}) collective-permute-start(f32[256,2,256]{2,0,1:T(8,128)} %bitcast.32), channel_id=1, source_target_pairs={{0,2},{1,3},{2,0},{3,1},{4,6},{5,7},{6,4},{7,5},{8,10},{9,11},{10,... | collective-permute-start | bytes 1572872 | tf_op jit(solution)/shard_map/ppermute | solution.py:129
  87.4 47.1 %collective-permute-start.2 = (f32[256,2,256]{2,0,1:T(8,128)}, f32[256,2,256]{2,0,1:T(8,128)}, u32[]{:S(2)}, u32[]{:S(2)}) collective-permute-start(f32[256,2,256]{2,0,1:T(8,128)} %bitcast.34), channel_id=1, source_target_pairs={{0,3},{1,2},{2,1},{3,0},{4,7},{5,6},{6,5},{7,4},{8,11},{9,10},{10,... | collective-permute-start | bytes 1572872 | tf_op jit(solution)/shard_map/ppermute | solution.py:129
  88.8 47.6 %collective-permute-start.3 = (f32[256,2,256]{2,0,1:T(8,128)}, f32[256,2,256]{2,0,1:T(8,128)}, u32[]{:S(2)}, u32[]{:S(2)}) collective-permute-start(f32[256,2,256]{2,0,1:T(8,128)} %bitcast.36), channel_id=1, source_target_pairs={{0,4},{1,5},{2,6},{3,7},{4,0},{5,1},{6,2},{7,3},{8,12},{9,13},{10,... | collective-permute-start | bytes 1572872 | tf_op jit(solution)/shard_map/ppermute | solution.py:129
  91.1 12.9 %copy-start.9 = (s32[4096]{0:T(1024)S(1)}, s32[4096]{0:T(1024)}, u32[]{:S(2)}) copy-start(s32[4096]{0:T(1024)} %param.7) | copy-start | bytes 49156
  91.1 49.9 %collective-permute-start.4 = (f32[256,2,256]{2,0,1:T(8,128)}, f32[256,2,256]{2,0,1:T(8,128)}, u32[]{:S(2)}, u32[]{:S(2)}) collective-permute-start(f32[256,2,256]{2,0,1:T(8,128)} %bitcast.38), channel_id=1, source_target_pairs={{0,5},{1,4},{2,7},{3,6},{4,1},{5,0},{6,3},{7,2},{8,13},{9,12},{10,... | collective-permute-start | bytes 1572872 | tf_op jit(solution)/shard_map/ppermute | solution.py:129
  104.0 2.6 copy-start.2
  104.0 3.7 copy-start.3
  107.8 18.4 %copy-start.8 = (f32[256,2,1,256]{0,3,2,1:T(8,128)S(1)}, f32[256,2,1,256]{0,3,2,1:T(8,128)}, u32[]{:S(2)}) copy-start(f32[256,2,1,256]{0,3,2,1:T(8,128)} %get-tuple-element.47) | copy-start | bytes 1572868
  117.4 9.8 %copy-start.7 = (f32[256,2,1,256]{0,3,2,1:T(8,128)S(1)}, f32[256,2,1,256]{0,3,2,1:T(8,128)}, u32[]{:S(2)}) copy-start(f32[256,2,1,256]{0,3,2,1:T(8,128)} %get-tuple-element.46) | copy-start | bytes 1572868
  117.4 10.0 %copy-start.6 = (f32[256,2,1,256]{0,3,2,1:T(8,128)S(1)}, f32[256,2,1,256]{0,3,2,1:T(8,128)}, u32[]{:S(2)}) copy-start(f32[256,2,1,256]{0,3,2,1:T(8,128)} %get-tuple-element.45) | copy-start | bytes 1572868
  117.4 10.2 %copy-start.5 = (f32[256,2,1,256]{0,3,2,1:T(8,128)S(1)}, f32[256,2,1,256]{0,3,2,1:T(8,128)}, u32[]{:S(2)}) copy-start(f32[256,2,1,256]{0,3,2,1:T(8,128)} %get-tuple-element.44) | copy-start | bytes 1572868
  117.4 10.4 %copy-start.4 = (f32[256,2,1,256]{0,3,2,1:T(8,128)S(1)}, f32[256,2,1,256]{0,3,2,1:T(8,128)}, u32[]{:S(2)}) copy-start(f32[256,2,1,256]{0,3,2,1:T(8,128)} %get-tuple-element.43) | copy-start | bytes 1572868
  128.2 30.1 %collective-permute-start.5 = (f32[256,2,256]{2,0,1:T(8,128)}, f32[256,2,256]{2,0,1:T(8,128)S(1)}, u32[]{:S(2)}, u32[]{:S(2)}) collective-permute-start(f32[256,2,256]{2,0,1:T(8,128)} %bitcast.213), channel_id=1, source_target_pairs={{0,6},{1,7},{2,4},{3,5},{4,2},{5,3},{6,0},{7,1},{8,14},{9,15},{10,... | collective-permute-start | bytes 1572872 | tf_op jit(solution)/shard_map/ppermute | solution.py:129
  132.4 37.1 %collective-permute-start.6 = (f32[256,2,256]{2,0,1:T(8,128)}, f32[256,2,256]{2,0,1:T(8,128)S(1)}, u32[]{:S(2)}, u32[]{:S(2)}) collective-permute-start(f32[256,2,256]{2,0,1:T(8,128)} %bitcast.212), channel_id=1, source_target_pairs={{0,7},{1,6},{2,5},{3,4},{4,3},{5,2},{6,1},{7,0},{8,15},{9,14},{10,... | collective-permute-start | bytes 1572872 | tf_op jit(solution)/shard_map/ppermute | solution.py:129
  134.5 37.1 %collective-permute-start.7 = (f32[256,2,256]{2,0,1:T(8,128)}, f32[256,2,256]{2,0,1:T(8,128)S(1)}, u32[]{:S(2)}, u32[]{:S(2)}) collective-permute-start(f32[256,2,256]{2,0,1:T(8,128)} %bitcast.211), channel_id=1, source_target_pairs={{0,8},{1,9},{2,10},{3,11},{4,12},{5,13},{6,14},{7,15},{8,0},{9,1},... | collective-permute-start | bytes 1572872 | tf_op jit(solution)/shard_map/ppermute | solution.py:129
  136.4 88.3 %collective-permute-start.8 = (f32[256,2,256]{2,0,1:T(8,128)}, f32[256,2,256]{2,0,1:T(8,128)S(1)}, u32[]{:S(2)}, u32[]{:S(2)}) collective-permute-start(f32[256,2,256]{2,0,1:T(8,128)} %bitcast.210), channel_id=1, source_target_pairs={{0,9},{1,8},{2,11},{3,10},{4,13},{5,12},{6,15},{7,14},{8,1},{9,0},... | collective-permute-start | bytes 1572872 | tf_op jit(solution)/shard_map/ppermute | solution.py:129
  141.0 106.2 %collective-permute-start.9 = (f32[256,2,256]{2,0,1:T(8,128)}, f32[256,2,256]{2,0,1:T(8,128)S(1)}, u32[]{:S(2)}, u32[]{:S(2)}) collective-permute-start(f32[256,2,256]{2,0,1:T(8,128)} %bitcast.208), channel_id=1, source_target_pairs={{0,10},{1,11},{2,8},{3,9},{4,14},{5,15},{6,12},{7,13},{8,2},{9,3},... | collective-permute-start | bytes 1572872 | tf_op jit(solution)/shard_map/ppermute | solution.py:129
  158.3 111.3 %collective-permute-start.10 = (f32[256,2,256]{2,0,1:T(8,128)S(1)}, f32[256,2,256]{2,0,1:T(8,128)S(1)}, u32[]{:S(2)}, u32[]{:S(2)}) collective-permute-start(f32[256,2,256]{2,0,1:T(8,128)S(1)} %bitcast.207), channel_id=1, source_target_pairs={{0,11},{1,10},{2,9},{3,8},{4,15},{5,14},{6,13},{7,12},{8,3},{9,2},... | collective-permute-start | bytes 1572872 | tf_op jit(solution)/shard_map/ppermute | solution.py:129
  169.5 114.4 %collective-permute-start.11 = (f32[256,2,256]{2,0,1:T(8,128)S(1)}, f32[256,2,256]{2,0,1:T(8,128)S(1)}, u32[]{:S(2)}, u32[]{:S(2)}) collective-permute-start(f32[256,2,256]{2,0,1:T(8,128)S(1)} %bitcast.206), channel_id=1, source_target_pairs={{0,12},{1,13},{2,14},{3,15},{4,8},{5,9},{6,10},{7,11},{8,4},{9,5},... | collective-permute-start | bytes 1572872 | tf_op jit(solution)/shard_map/ppermute | solution.py:129
  171.7 124.5 %collective-permute-start.12 = (f32[256,2,256]{2,0,1:T(8,128)S(1)}, f32[256,2,256]{2,0,1:T(8,128)S(1)}, u32[]{:S(2)}, u32[]{:S(2)}) collective-permute-start(f32[256,2,256]{2,0,1:T(8,128)S(1)} %bitcast.205), channel_id=1, source_target_pairs={{0,13},{1,12},{2,15},{3,14},{4,9},{5,8},{6,11},{7,10},{8,5},{9,4},... | collective-permute-start | bytes 1572872 | tf_op jit(solution)/shard_map/ppermute | solution.py:129
  224.7 82.6 %collective-permute-start.13 = (f32[256,2,256]{2,0,1:T(8,128)S(1)}, f32[256,2,256]{2,0,1:T(8,128)S(1)}, u32[]{:S(2)}, u32[]{:S(2)}) collective-permute-start(f32[256,2,256]{2,0,1:T(8,128)S(1)} %bitcast.204), channel_id=1, source_target_pairs={{0,14},{1,15},{2,12},{3,13},{4,10},{5,11},{6,8},{7,9},{8,6},{9,7},... | collective-permute-start | bytes 1572872 | tf_op jit(solution)/shard_map/ppermute | solution.py:129
  247.2 71.7 %collective-permute-start.14 = (f32[256,2,256]{2,0,1:T(8,128)S(1)}, f32[256,2,256]{2,0,1:T(8,128)S(1)}, u32[]{:S(2)}, u32[]{:S(2)}) collective-permute-start(f32[256,2,256]{2,0,1:T(8,128)S(1)} %bitcast.203), channel_id=1, source_target_pairs={{0,15},{1,14},{2,13},{3,12},{4,11},{5,10},{6,9},{7,8},{8,7},{9,6},... | collective-permute-start | bytes 1572872 | tf_op jit(solution)/shard_map/ppermute | solution.py:129
  344.7 22.1 %copy-start.1 = (f32[64,64,256]{2,0,1:T(8,128)S(1)}, f32[64,64,256]{2,0,1:T(8,128)}, u32[]{:S(2)}) copy-start(f32[64,64,256]{2,0,1:T(8,128)} %compare_convert_fusion) | copy-start | bytes 12582916
  433.5 186.0 %all-to-all-start = ((f32[4096,2,256]{2,1,0:T(2,128)}), f32[4096,2,256]{2,1,0:T(2,128)}, u32[]{:S(2)}, u32[]{:S(2)}) async-start(f32[4096,2,256]{2,1,0:T(2,128)} %copy.157), calls=%async_computation | async-start | bytes 16777216 | tf_op jit(solution)/shard_map/all_to_all | solution.py:140
  697.2 18.8 %copy-start.10 = (f32[8,32]{1,0:T(8,128)S(1)}, f32[8,32]{1,0:T(8,128)}, u32[]{:S(2)}) copy-start(f32[8,32]{1,0:T(8,128)} %param.9) | copy-start | bytes 3076
  697.2 18.8 %copy-start.11 = (s32[8,32]{1,0:T(8,128)S(1)}, s32[8,32]{1,0:T(8,128)}, u32[]{:S(2)}) copy-start(s32[8,32]{1,0:T(8,128)} %param.8) | copy-start | bytes 3076
  709.1 2.0 copy-start
  711.2 13.8 %collective-permute-start.15 = (bf16[31,8192]{1,0:T(8,128)(2,1)S(1)}, bf16[31,8192]{1,0:T(8,128)(2,1)S(1)}, u32[]{:S(2)}, u32[]{:S(2)}) collective-permute-start(bf16[31,8192]{1,0:T(8,128)(2,1)S(1)} %get-tuple-element.58), channel_id=1, source_target_pairs={{0,1},{1,2},{2,3},{3,4},{4,5},{5,6},{6,7},{7,8},{8,9},{9,10},{10,1... | collective-permute-start | bytes 1523720 | tf_op jit(solution)/shard_map/ppermute | solution.py:31
  713.3 15.2 %collective-permute-start.16 = (bf16[31,8192]{1,0:T(8,128)(2,1)S(1)}, bf16[31,8192]{1,0:T(8,128)(2,1)S(1)}, u32[]{:S(2)}, u32[]{:S(2)}) collective-permute-start(bf16[31,8192]{1,0:T(8,128)(2,1)S(1)} %get-tuple-element.59), channel_id=1, source_target_pairs={{1,0},{2,1},{3,2},{4,3},{5,4},{6,5},{7,6},{8,7},{9,8},{10,9},{11,1... | collective-permute-start | bytes 1523720 | tf_op jit(solution)/shard_map/ppermute | solution.py:32
